TPU v7x, 512 devices: a whole 4x4x16 slice. The times are simulated.
512 devices in a mesh: gx: 32 (over x, y, core), gy: 16 (over z).
Axes of the slice: x: 4, y: 4, z: 16, core: 2. Of those that a mesh axis runs over, the one named last changes fastest.
Arguments:
- conductance: float32 [16, 256, 2048], P(None, 'gx', 'gy'), may hold values from 0.2 to 5
- labels: int32 [16, 256, 2048], P(None, 'gx', 'gy'), may hold values from 0 to 2, as said below
- cotangent: float32 [2, 16, 256, 2048], P(None, None, 'gx', 'gy')
- saved: float32 [2, 16, 256, 2048], P(None, None, 'gx', 'gy'), may hold values from 0 to 1
Outputs:
- adjoint: float32 [2, 16, 256, 2048], P(None, None, 'gx', 'gy')
- gradient: float32 [16, 256, 2048], P(None, 'gx', 'gy')
Inputs may be any that keep to these rules, and one draw needn't show every extreme that they name: `labels`: 0 marks an unseeded voxel, 1 or 2 the class of a seed.
All inputs are finite; a program needn't handle non-finite values.
Results may differ from a plain program's by a relative error of at most 0.0003.
Values sent between devices are 32-bit elements; how exact they have to be, the bound alone decides.
No kernel may reach another device: no remote copies, remote signals or barrier semaphores. Data moves between devices by JAX's collectives and lax.ppermute only.
A program may use at most 64 MiB of HBM per device.

v0:
```python
import jax
import jax.numpy as jnp
from jax import lax
from jax.sharding import PartitionSpec as P

ITERS = 3
prior_strength = 1.0


def extended(x, sides, width):
    for axis, dim in sides:
        size, length = (lax.axis_size(axis), x.shape[dim])
        up = [(i, (i + 1) % size) for i in range(size - 1)]
        down = [(j, i) for i, j in up]
        last = lax.slice_in_dim(x, length - width, length, axis=dim)
        initial = lax.slice_in_dim(x, 0, width, axis=dim)
        before = lax.ppermute(last, axis, up)
        after = lax.ppermute(initial, axis, down)
        x = jnp.concatenate([before, x, after], axis=dim)
    return x


def potentials(labels, saved):
    classes = jnp.arange(1, 3, dtype=jnp.int32)[:, None, None, None]
    tagged = labels[None]
    return jnp.where(tagged == classes, 1.0, jnp.where(tagged > 0, 0.0, saved))


def edge_validity(row_count, col_count, depth):
    row_pos = lax.axis_index("gx") * row_count + jnp.arange(row_count, dtype=jnp.int32)
    col_pos = lax.axis_index("gy") * col_count + jnp.arange(col_count, dtype=jnp.int32)
    depth_pos = jnp.arange(depth, dtype=jnp.int32)
    total_rows = row_count * lax.axis_size("gx")
    total_cols = col_count * lax.axis_size("gy")
    return (
        (row_pos > 0).astype(jnp.float32)[None, :, None],
        (row_pos < total_rows - 1).astype(jnp.float32)[None, :, None],
        (col_pos > 0).astype(jnp.float32)[None, None, :],
        (col_pos < total_cols - 1).astype(jnp.float32)[None, None, :],
        (depth_pos > 0).astype(jnp.float32)[:, None, None],
        (depth_pos < depth - 1).astype(jnp.float32)[:, None, None],
    )


def side_slices(padded):
    return (
        padded[..., :-2, 1:-1],
        padded[..., 2:, 1:-1],
        padded[..., 1:-1, :-2],
        padded[..., 1:-1, 2:],
    )


def depth_neighbours(input_vector):
    depth_axis = input_vector.ndim - 3
    depth = input_vector.shape[depth_axis]
    widths = [(0, 0)] * input_vector.ndim
    widths[depth_axis] = (1, 1)
    padded = jnp.pad(input_vector, widths)
    lower = lax.slice_in_dim(padded, 0, depth, axis=depth_axis)
    upper = lax.slice_in_dim(padded, 2, depth + 2, axis=depth_axis)
    return (lower, upper)


def apply_operator(input_vector, unlabelled_mask, weight_field):
    mask_applied = unlabelled_mask * input_vector
    padded = extended(mask_applied, (("gx", 2), ("gy", 3)), 1)
    neighbours = side_slices(padded) + depth_neighbours(mask_applied)
    graph_laplacian = jnp.zeros_like(mask_applied)
    for weight, neighbour in zip(weight_field, neighbours):
        graph_laplacian = graph_laplacian + weight * (mask_applied - neighbour)
    return (
        unlabelled_mask * (prior_strength * mask_applied + graph_laplacian)
        + (1.0 - unlabelled_mask) * input_vector
    )


def class_sum(first_vec, second_vec):
    return jnp.sum(first_vec * second_vec, axis=(1, 2, 3))


def expand(scalars):
    return scalars[:, None, None, None]


def global_norm(solver_residual):
    return lax.psum(class_sum(solver_residual, solver_residual), ("gx", "gy"))


def per_device(conductance, labels, cotangent, saved):
    depth, row_count, col_count = conductance.shape
    validity = edge_validity(row_count, col_count, depth)
    potential = potentials(labels, saved)
    unlabelled_mask = (labels == 0).astype(jnp.float32)[None]
    solver_residual = unlabelled_mask * cotangent
    cond_pad = extended(conductance, (("gx", 1), ("gy", 2)), 1)
    cond_neighbours = side_slices(cond_pad) + depth_neighbours(conductance)
    weight_field = [
        0.5 * (conductance + neighbour) * valid_edge
        for neighbour, valid_edge in zip(cond_neighbours, validity)
    ]
    adjoint = jnp.zeros_like(solver_residual)
    search_direction = solver_residual
    norm_now = global_norm(solver_residual)
    for iteration in range(ITERS):
        operator_result = apply_operator(search_direction, unlabelled_mask, weight_field)
        step_size = norm_now / lax.psum(class_sum(search_direction, operator_result), ("gx", "gy"))
        adjoint = adjoint + expand(step_size) * search_direction
        solver_residual = solver_residual - expand(step_size) * operator_result
        if iteration + 1 < ITERS:
            norm_next = global_norm(solver_residual)
            search_direction = solver_residual + expand(norm_next / norm_now) * search_direction
            norm_now = norm_next
    joined = extended(jnp.concatenate((adjoint, potential), axis=0), (("gx", 2), ("gy", 3)), 1)
    adj_pad = joined[:2]
    pot_pad = joined[2:]
    adj_neighbours = side_slices(adj_pad) + depth_neighbours(adjoint)
    pot_neighbours = side_slices(pot_pad) + depth_neighbours(potential)
    gradient = jnp.zeros_like(conductance)
    for adj_nb, pot_nb, valid_edge in zip(adj_neighbours, pot_neighbours, validity):
        gradient = (
            gradient - jnp.sum((adjoint - adj_nb) * (potential - pot_nb), axis=0) * valid_edge
        )
    return (adjoint, 0.5 * gradient)


def solution(mesh):
    return jax.shard_map(
        per_device,
        mesh=mesh,
        in_specs=(
            P(None, "gx", "gy"),
            P(None, "gx", "gy"),
            P(None, None, "gx", "gy"),
            P(None, None, "gx", "gy"),
        ),
        out_specs=(P(None, None, "gx", "gy"), P(None, "gx", "gy")),
        check_vma=False,
    )
```

profile of v0, /device:TPU:1, one launch (start us, length us, event | category | flops | bytes accessed | tf_op | source)
XLA Modules:
  0.0 619.8 jit_solution(12101957498100516942)
XLA Ops:
  1.6 4.7 collective-permute-start.1
  6.4 5.5 collective-permute-start.3
  11.9 1.9 collective-permute-start
  13.8 2.4 collective-permute-start.2
  16.4 2.4 collective-permute-done.2
  18.9 1.7 collective-permute-start.4
  22.1 4.2 collective-permute-start.5
  27.8 3.5 collective-permute-done.5
  31.4 4.1 collective-permute-done.7
  35.9 112.1 %all-reduce.6 = (f32[2]{0:T(128)S(1)}, f32[2]{0:T(128)S(1)}) all-reduce(f32[2]{0:T(128)S(1)} %get-tuple-element.9, f32[2]{0:T(128)S(1)} %get-tuple-element.8), channel_id=1, replica_groups=mesh['gx'=32,'gy'=16] {'gx','gy'}, use_global_device_ids=true, to_apply=%region_1.2 | all-reduce | flops 4 | bytes 32 | tf_op jit(solution)/shard_map/psum | solution.py:87
  148.2 98.7 %psum.44 = f32[2]{0:T(128)S(1)} all-reduce(f32[2]{0:T(128)S(1)} %get-tuple-element.18), channel_id=1, replica_groups=mesh['gx'=32,'gy'=16] {'gx','gy'}, use_global_device_ids=true, to_apply=%region_5.6 | all-reduce | flops 2 | bytes 16 | tf_op jit(solution)/shard_map/psum | solution.py:87
  246.9 3.4 collective-permute-start.8
  250.4 1.9 collective-permute-start.9
  252.3 3.1 collective-permute-done.9
  255.6 3.7 collective-permute-start.10
  260.6 3.3 collective-permute-done.10
  263.9 4.1 collective-permute-done.11
  268.4 101.5 %psum.45 = f32[2]{0:T(128)S(1)} all-reduce(f32[2]{0:T(128)S(1)} %get-tuple-element.14), channel_id=1, replica_groups=mesh['gx'=32,'gy'=16] {'gx','gy'}, use_global_device_ids=true, to_apply=%region_7.8 | all-reduce | flops 2 | bytes 16 | tf_op jit(solution)/shard_map/psum | solution.py:107
  370.1 99.5 %psum.46 = f32[2]{0:T(128)S(1)} all-reduce(f32[2]{0:T(128)S(1)} %multiply_reduce_fusion), channel_id=1, replica_groups=mesh['gx'=32,'gy'=16] {'gx','gy'}, use_global_device_ids=true, to_apply=%region_9.10 | all-reduce | flops 2 | bytes 16 | tf_op jit(solution)/shard_map/psum | solution.py:87
  469.7 3.5 collective-permute-start.12
  473.2 1.9 collective-permute-start.13
  475.3 3.0 collective-permute-done.13
  478.5 3.7 collective-permute-start.14
  483.5 3.3 collective-permute-done.14
  486.8 4.1 collective-permute-done.15
  491.3 101.5 %psum.47 = f32[2]{0:T(128)S(1)} all-reduce(f32[2]{0:T(128)S(1)} %fusion.81), channel_id=1, replica_groups=mesh['gx'=32,'gy'=16] {'gx','gy'}, use_global_device_ids=true, to_apply=%region_11.12 | all-reduce | flops 2 | bytes 16 | tf_op jit(solution)/shard_map/psum | solution.py:107
  592.9 3.7 collective-permute-start.16
  596.6 1.9 collective-permute-start.17
  598.6 3.3 collective-permute-done.17
  602.2 2.4 collective-permute-start.18
  605.9 8.7 %collective-permute-done.18 = f32[4,16,10,1]{3,2,1,0:T(8,128)S(1)} collective-permute-done((f32[4,16,10,1]{3,2,1,0:T(8,128)S(1)}, f32[4,16,10,1]{3,2,1,0:T(8,128)S(1)}, u32[]{:S(2)}, u32[]{:S(2)}) %collective-permute-start.18) | collective-permute-done | bytes 2592 | tf_op jit(solution)/shard_map/ppermute | solution.py:17
  614.8 4.0 collective-permute-done.19
  (68 shorter events, 11.9 us)
Async XLA Ops:
  0.6 0.9 copy-start.1
  1.6 14.7 %copy-start.3 = (s32[16,8,128]{2,1,0:T(8,128)S(1)}, s32[16,8,128]{2,1,0:T(8,128)}, u32[]{:S(2)}) copy-start(s32[16,8,128]{2,1,0:T(8,128)} %param.5) | copy-start | bytes 196612
  1.6 10.3 %copy-start.2 = (f32[16,8,128]{2,1,0:T(8,128)S(1)}, f32[16,8,128]{2,1,0:T(8,128)}, u32[]{:S(2)}) copy-start(f32[16,8,128]{2,1,0:T(8,128)} %param.4) | copy-start | bytes 196612
  1.6 20.3 %collective-permute-start.1 = (f32[2,16,1,128]{3,2,1,0:T(1,128)S(1)}, f32[2,16,1,128]{3,2,1,0:T(1,128)S(1)}, u32[]{:S(2)}, u32[]{:S(2)}) collective-permute-start(f32[2,16,1,128]{3,2,1,0:T(1,128)S(1)} %get-tuple-element.37), channel_id=1, source_target_pairs={{0,16},{16,32},{32,48},{48,64},{64,80},{80,96},{96,112},{112,128},... | collective-permute-start | bytes 49160 | tf_op jit(solution)/shard_map/ppermute | solution.py:17
  6.4 15.6 %collective-permute-start.3 = (f32[2,16,1,128]{3,2,1,0:T(1,128)S(1)}, f32[2,16,1,128]{3,2,1,0:T(1,128)S(1)}, u32[]{:S(2)}, u32[]{:S(2)}) collective-permute-start(f32[2,16,1,128]{3,2,1,0:T(1,128)S(1)} %get-tuple-element.38), channel_id=1, source_target_pairs={{16,0},{32,16},{48,32},{64,48},{80,64},{96,80},{112,96},{128,112},... | collective-permute-start | bytes 49160 | tf_op jit(solution)/shard_map/ppermute | solution.py:18
  11.9 4.5 collective-permute-start
  13.8 5.0 collective-permute-start.2
  18.9 8.7 %collective-permute-start.4 = (f32[16,10,1]{2,1,0:T(8,128)S(1)}, f32[16,10,1]{2,1,0:T(8,128)S(1)}, u32[]{:S(2)}, u32[]{:S(2)}) collective-permute-start(f32[16,10,1]{2,1,0:T(8,128)S(1)} %get-tuple-element.35), channel_id=1, source_target_pairs={{0,1},{1,2},{2,3},{3,4},{4,5},{5,6},{6,7},{7,8},{8,9},{9,10},{10,1... | collective-permute-start | bytes 1928 | tf_op jit(solution)/shard_map/ppermute | solution.py:17
  20.6 7.0 %collective-permute-start.6 = (f32[16,10,1]{2,1,0:T(8,128)S(1)}, f32[16,10,1]{2,1,0:T(8,128)S(1)}, u32[]{:S(2)}, u32[]{:S(2)}) collective-permute-start(f32[16,10,1]{2,1,0:T(8,128)S(1)} %get-tuple-element.36), channel_id=1, source_target_pairs={{1,0},{2,1},{3,2},{4,3},{5,4},{6,5},{7,6},{8,7},{9,8},{10,9},{11,1... | collective-permute-start | bytes 1928 | tf_op jit(solution)/shard_map/ppermute | solution.py:18
  22.1 9.2 %collective-permute-start.5 = (f32[2,16,10,1]{3,2,1,0:T(8,128)S(1)}, f32[2,16,10,1]{3,2,1,0:T(8,128)S(1)}, u32[]{:S(2)}, u32[]{:S(2)}) collective-permute-start(f32[2,16,10,1]{3,2,1,0:T(8,128)S(1)} %get-tuple-element.29), channel_id=1, source_target_pairs={{0,1},{1,2},{2,3},{3,4},{4,5},{5,6},{6,7},{7,8},{8,9},{9,10},{10,1... | collective-permute-start | bytes 3848 | tf_op jit(solution)/shard_map/ppermute | solution.py:17
  26.3 9.2 %collective-permute-start.7 = (f32[2,16,10,1]{3,2,1,0:T(8,128)S(1)}, f32[2,16,10,1]{3,2,1,0:T(8,128)S(1)}, u32[]{:S(2)}, u32[]{:S(2)}) collective-permute-start(f32[2,16,10,1]{3,2,1,0:T(8,128)S(1)} %get-tuple-element.30), channel_id=1, source_target_pairs={{1,0},{2,1},{3,2},{4,3},{5,4},{6,5},{7,6},{8,7},{9,8},{10,9},{11,1... | collective-permute-start | bytes 3848 | tf_op jit(solution)/shard_map/ppermute | solution.py:18
  246.9 5.4 collective-permute-start.8
  250.4 5.1 collective-permute-start.9
  255.6 8.3 %collective-permute-start.10 = (f32[2,16,10,1]{3,2,1,0:T(8,128)S(1)}, f32[2,16,10,1]{3,2,1,0:T(8,128)S(1)}, u32[]{:S(2)}, u32[]{:S(2)}) collective-permute-start(f32[2,16,10,1]{3,2,1,0:T(8,128)S(1)} %get-tuple-element.27), channel_id=1, source_target_pairs={{0,1},{1,2},{2,3},{3,4},{4,5},{5,6},{6,7},{7,8},{8,9},{9,10},{10,1... | collective-permute-start | bytes 3848 | tf_op jit(solution)/shard_map/ppermute | solution.py:17
  259.3 8.7 %collective-permute-start.11 = (f32[2,16,10,1]{3,2,1,0:T(8,128)S(1)}, f32[2,16,10,1]{3,2,1,0:T(8,128)S(1)}, u32[]{:S(2)}, u32[]{:S(2)}) collective-permute-start(f32[2,16,10,1]{3,2,1,0:T(8,128)S(1)} %get-tuple-element.28), channel_id=1, source_target_pairs={{1,0},{2,1},{3,2},{4,3},{5,4},{6,5},{7,6},{8,7},{9,8},{10,9},{11,1... | collective-permute-start | bytes 3848 | tf_op jit(solution)/shard_map/ppermute | solution.py:18
  469.6 5.6 copy-start.4
  469.7 5.5 collective-permute-start.12
  473.2 5.1 collective-permute-start.13
  478.5 8.3 %collective-permute-start.14 = (f32[2,16,10,1]{3,2,1,0:T(8,128)S(1)}, f32[2,16,10,1]{3,2,1,0:T(8,128)S(1)}, u32[]{:S(2)}, u32[]{:S(2)}) collective-permute-start(f32[2,16,10,1]{3,2,1,0:T(8,128)S(1)} %get-tuple-element.25), channel_id=1, source_target_pairs={{0,1},{1,2},{2,3},{3,4},{4,5},{5,6},{6,7},{7,8},{8,9},{9,10},{10,1... | collective-permute-start | bytes 3848 | tf_op jit(solution)/shard_map/ppermute | solution.py:17
  482.2 8.7 %collective-permute-start.15 = (f32[2,16,10,1]{3,2,1,0:T(8,128)S(1)}, f32[2,16,10,1]{3,2,1,0:T(8,128)S(1)}, u32[]{:S(2)}, u32[]{:S(2)}) collective-permute-start(f32[2,16,10,1]{3,2,1,0:T(8,128)S(1)} %get-tuple-element.26), channel_id=1, source_target_pairs={{1,0},{2,1},{3,2},{4,3},{5,4},{6,5},{7,6},{8,7},{9,8},{10,9},{11,1... | collective-permute-start | bytes 3848 | tf_op jit(solution)/shard_map/ppermute | solution.py:18
  592.8 26.0 %copy-start = (f32[2,16,8,128]{3,2,1,0:T(8,128)}, f32[2,16,8,128]{3,2,1,0:T(8,128)S(1)}, u32[]{:S(2)}) copy-start(f32[2,16,8,128]{3,2,1,0:T(8,128)S(1)} %multiply_add_fusion) | copy-start | bytes 393220
  592.9 5.7 collective-permute-start.16
  596.6 5.2 collective-permute-start.17
  602.2 12.5 %collective-permute-start.18 = (f32[4,16,10,1]{3,2,1,0:T(8,128)S(1)}, f32[4,16,10,1]{3,2,1,0:T(8,128)S(1)}, u32[]{:S(2)}, u32[]{:S(2)}) collective-permute-start(f32[4,16,10,1]{3,2,1,0:T(8,128)S(1)} %get-tuple-element.21), channel_id=1, source_target_pairs={{0,1},{1,2},{2,3},{3,4},{4,5},{5,6},{6,7},{7,8},{8,9},{9,10},{10,1... | collective-permute-start | bytes 7688 | tf_op jit(solution)/shard_map/ppermute | solution.py:17
  604.6 14.2 %collective-permute-start.19 = (f32[4,16,10,1]{3,2,1,0:T(8,128)S(1)}, f32[4,16,10,1]{3,2,1,0:T(8,128)S(1)}, u32[]{:S(2)}, u32[]{:S(2)}) collective-permute-start(f32[4,16,10,1]{3,2,1,0:T(8,128)S(1)} %get-tuple-element.22), channel_id=1, source_target_pairs={{1,0},{2,1},{3,2},{4,3},{5,4},{6,5},{7,6},{8,7},{9,8},{10,9},{11,1... | collective-permute-start | bytes 7688 | tf_op jit(solution)/shard_map/ppermute | solution.py:18
where the time goes:
time: 621 us; the launch traced here: 620 us
  blocking collectives  513 us (83%)
  starting transfers between devices  53.1 us (9%)
  waiting for transfers between devices  46.9 us (8%)
    psum x3, blocking collectives, global_norm(): return lax.psum(class_sum(solver_residual, solver_residual), ('gx', 'gy'))  310 us
    psum x2, blocking collectives, per_device(): lax.psum(class_sum(search_direction, operator_result), ('gx', 'gy'))  203 us
    ppermute x10, starting transfers between devices, extended(): before = lax.ppermute(last, axis, up)  33 us
    ppermute x10, waiting for transfers between devices, extended(): after = lax.ppermute(initial, axis, down)  28.1 us
    ppermute x10, starting transfers between devices, extended(): after = lax.ppermute(initial, axis, down)  20.1 us
    ppermute x10, waiting for transfers between devices, extended(): before = lax.ppermute(last, axis, up)  18.8 us
  transfers between devices with their start and end apart: 20, of which 12 were waited for; matrix products, arithmetic and copies ran while one was open for 0% of the time, Pallas kernels for 0%

commit v1 on v0

--- a/solution.py
+++ b/solution.py
@@ -104,7 +104,9 @@
     norm_now = global_norm(solver_residual)
     for iteration in range(ITERS):
         operator_result = apply_operator(search_direction, unlabelled_mask, weight_field)
-        step_size = norm_now / lax.psum(class_sum(search_direction, operator_result), ("gx", "gy"))
+        step_size = norm_now / lax.psum(
+            lax.psum(class_sum(search_direction, operator_result), "gy"), "gx"
+        )
         adjoint = adjoint + expand(step_size) * search_direction
         solver_residual = solver_residual - expand(step_size) * operator_result
         if iteration + 1 < ITERS:

time: 621 us -> 682 us (1.098)
  blocking collectives: 513 us -> 580 us
    psum x2 -> x6, blocking collectives: 203 us -> 281 us  [the longest x3 206 us: per_device(): lax.psum(lax.psum(class_sum(search_direction, operator_result), 'gy'), 'gx')]
    psum x3, blocking collectives: 310 us -> 298 us  [global_norm(): return lax.psum(class_sum(solver_residual, solver_residual), ('gx', 'gy'))]
where the time goes in v1:
time: 682 us; the launch traced here: 680 us
  blocking collectives  580 us (85%)
  starting transfers between devices  47.2 us (7%)
  waiting for transfers between devices  46.9 us (7%)
    psum x3, blocking collectives, global_norm(): return lax.psum(class_sum(solver_residual, solver_residual), ('gx', 'gy'))  298 us
    psum x3, blocking collectives, per_device(): lax.psum(lax.psum(class_sum(search_direction, operator_result), 'gy'), 'gx')  206 us
    psum x3, blocking collectives, per_device(): lax.psum(class_sum(search_direction, operator_result), 'gy')  75.8 us
    ppermute x10, waiting for transfers between devices, extended(): after = lax.ppermute(initial, axis, down)  27.5 us
    ppermute x10, starting transfers between devices, extended(): before = lax.ppermute(last, axis, up)  26.4 us
    ppermute x10, starting transfers between devices, extended(): after = lax.ppermute(initial, axis, down)  20.8 us
    ppermute x10, waiting for transfers between devices, extended(): before = lax.ppermute(last, axis, up)  19.4 us
  transfers between devices with their start and end apart: 20, of which 12 were waited for; matrix products, arithmetic and copies ran while one was open for 0% of the time, Pallas kernels for 0%

profile of v1, /device:TPU:1, one launch (start us, length us, event | category | flops | bytes accessed | tf_op | source)
XLA Modules:
  0.0 680.2 jit_solution(550349070228046635)
XLA Ops:
  1.6 4.7 collective-permute-start.1
  6.4 5.5 collective-permute-start.3
  11.9 1.9 collective-permute-start
  13.8 2.4 collective-permute-start.2
  16.4 2.4 collective-permute-done.2
  22.1 4.2 collective-permute-start.5
  27.8 3.5 collective-permute-done.5
  31.4 4.1 collective-permute-done.7
  35.9 30.1 %psum.64 = f32[2]{0:T(128)S(1)} all-reduce(f32[2]{0:T(128)S(1)} %get-tuple-element.8), channel_id=1, replica_groups=mesh['gx'=32,'gy'=16] {'gy'}, use_global_device_ids=true, to_apply=%region_3.4 | all-reduce | flops 2 | bytes 16 | tf_op jit(solution)/shard_map/psum | solution.py:108
  66.0 68.8 %psum.65 = f32[2]{0:T(128)S(1)} all-reduce(f32[2]{0:T(128)S(1)} %psum.64), channel_id=1, replica_groups=mesh['gx'=32,'gy'=16] {'gx'}, use_global_device_ids=true, to_apply=%region_4.5 | all-reduce | flops 2 | bytes 16 | tf_op jit(solution)/shard_map/psum | solution.py:107
  134.8 98.7 %psum.63 = f32[2]{0:T(128)S(1)} all-reduce(f32[2]{0:T(128)S(1)} %get-tuple-element.9), channel_id=1, replica_groups=mesh['gx'=32,'gy'=16] {'gx','gy'}, use_global_device_ids=true, to_apply=%region_1.2 | all-reduce | flops 2 | bytes 16 | tf_op jit(solution)/shard_map/psum | solution.py:87
  233.7 100.7 %psum.66 = f32[2]{0:T(128)S(1)} all-reduce(f32[2]{0:T(128)S(1)} %get-tuple-element.16), channel_id=1, replica_groups=mesh['gx'=32,'gy'=16] {'gx','gy'}, use_global_device_ids=true, to_apply=%region_6.7 | all-reduce | flops 2 | bytes 16 | tf_op jit(solution)/shard_map/psum | solution.py:87
  334.5 2.9 collective-permute-start.8
  337.4 1.9 collective-permute-start.9
  339.4 3.1 collective-permute-done.9
  345.8 3.3 collective-permute-done.10
  349.0 4.1 collective-permute-done.11
  353.5 23.6 %psum.67 = f32[2]{0:T(128)S(1)} all-reduce(f32[2]{0:T(128)S(1)} %get-tuple-element.12), channel_id=1, replica_groups=mesh['gx'=32,'gy'=16] {'gy'}, use_global_device_ids=true, to_apply=%region_8.9 | all-reduce | flops 2 | bytes 16 | tf_op jit(solution)/shard_map/psum | solution.py:108
  377.1 68.0 %psum.68 = f32[2]{0:T(128)S(1)} all-reduce(f32[2]{0:T(128)S(1)} %psum.67), channel_id=1, replica_groups=mesh['gx'=32,'gy'=16] {'gx'}, use_global_device_ids=true, to_apply=%region_9.10 | all-reduce | flops 2 | bytes 16 | tf_op jit(solution)/shard_map/psum | solution.py:107
  445.2 98.7 %psum.69 = f32[2]{0:T(128)S(1)} all-reduce(f32[2]{0:T(128)S(1)} %multiply_reduce_fusion), channel_id=1, replica_groups=mesh['gx'=32,'gy'=16] {'gx','gy'}, use_global_device_ids=true, to_apply=%region_11.12 | all-reduce | flops 2 | bytes 16 | tf_op jit(solution)/shard_map/psum | solution.py:87
  544.1 2.2 collective-permute-start.12
  546.3 2.1 collective-permute-start.13
  548.4 2.9 collective-permute-done.13
  551.5 3.7 collective-permute-start.14
  556.6 3.4 collective-permute-done.14
  560.0 4.1 collective-permute-done.15
  564.5 22.1 %psum.70 = f32[2]{0:T(128)S(1)} all-reduce(f32[2]{0:T(128)S(1)} %fusion.81), channel_id=1, replica_groups=mesh['gx'=32,'gy'=16] {'gy'}, use_global_device_ids=true, to_apply=%region_13.14 | all-reduce | flops 2 | bytes 16 | tf_op jit(solution)/shard_map/psum | solution.py:108
  586.7 68.8 %psum.71 = f32[2]{0:T(128)S(1)} all-reduce(f32[2]{0:T(128)S(1)} %psum.70), channel_id=1, replica_groups=mesh['gx'=32,'gy'=16] {'gx'}, use_global_device_ids=true, to_apply=%region_14.15 | all-reduce | flops 2 | bytes 16 | tf_op jit(solution)/shard_map/psum | solution.py:107
  657.6 2.4 collective-permute-start.17
  660.0 2.8 collective-permute-done.17
  665.9 9.2 %collective-permute-done.18 = f32[4,16,10,1]{3,2,1,0:T(8,128)S(1)} collective-permute-done((f32[4,16,10,1]{3,2,1,0:T(8,128)S(1)}, f32[4,16,10,1]{3,2,1,0:T(8,128)S(1)}, u32[]{:S(2)}, u32[]{:S(2)}) %collective-permute-start.18) | collective-permute-done | bytes 2592 | tf_op jit(solution)/shard_map/ppermute | solution.py:17
  675.3 4.0 collective-permute-done.19
  (72 shorter events, 18.7 us)
Async XLA Ops:
  0.6 0.9 copy-start.1
  1.6 14.7 %copy-start.3 = (s32[16,8,128]{2,1,0:T(8,128)S(1)}, s32[16,8,128]{2,1,0:T(8,128)}, u32[]{:S(2)}) copy-start(s32[16,8,128]{2,1,0:T(8,128)} %param.5) | copy-start | bytes 196612
  1.6 10.3 %copy-start.2 = (f32[16,8,128]{2,1,0:T(8,128)S(1)}, f32[16,8,128]{2,1,0:T(8,128)}, u32[]{:S(2)}) copy-start(f32[16,8,128]{2,1,0:T(8,128)} %param.4) | copy-start | bytes 196612
  1.6 20.3 %collective-permute-start.1 = (f32[2,16,1,128]{3,2,1,0:T(1,128)S(1)}, f32[2,16,1,128]{3,2,1,0:T(1,128)S(1)}, u32[]{:S(2)}, u32[]{:S(2)}) collective-permute-start(f32[2,16,1,128]{3,2,1,0:T(1,128)S(1)} %get-tuple-element.35), channel_id=1, source_target_pairs={{0,16},{16,32},{32,48},{48,64},{64,80},{80,96},{96,112},{112,128},... | collective-permute-start | bytes 49160 | tf_op jit(solution)/shard_map/ppermute | solution.py:17
  6.4 15.6 %collective-permute-start.3 = (f32[2,16,1,128]{3,2,1,0:T(1,128)S(1)}, f32[2,16,1,128]{3,2,1,0:T(1,128)S(1)}, u32[]{:S(2)}, u32[]{:S(2)}) collective-permute-start(f32[2,16,1,128]{3,2,1,0:T(1,128)S(1)} %get-tuple-element.36), channel_id=1, source_target_pairs={{16,0},{32,16},{48,32},{64,48},{80,64},{96,80},{112,96},{128,112},... | collective-permute-start | bytes 49160 | tf_op jit(solution)/shard_map/ppermute | solution.py:18
  11.9 4.5 collective-permute-start
  13.8 5.0 collective-permute-start.2
  18.9 8.7 %collective-permute-start.4 = (f32[16,10,1]{2,1,0:T(8,128)S(1)}, f32[16,10,1]{2,1,0:T(8,128)S(1)}, u32[]{:S(2)}, u32[]{:S(2)}) collective-permute-start(f32[16,10,1]{2,1,0:T(8,128)S(1)} %get-tuple-element.33), channel_id=1, source_target_pairs={{0,1},{1,2},{2,3},{3,4},{4,5},{5,6},{6,7},{7,8},{8,9},{9,10},{10,1... | collective-permute-start | bytes 1928 | tf_op jit(solution)/shard_map/ppermute | solution.py:17
  20.6 7.0 %collective-permute-start.6 = (f32[16,10,1]{2,1,0:T(8,128)S(1)}, f32[16,10,1]{2,1,0:T(8,128)S(1)}, u32[]{:S(2)}, u32[]{:S(2)}) collective-permute-start(f32[16,10,1]{2,1,0:T(8,128)S(1)} %get-tuple-element.34), channel_id=1, source_target_pairs={{1,0},{2,1},{3,2},{4,3},{5,4},{6,5},{7,6},{8,7},{9,8},{10,9},{11,1... | collective-permute-start | bytes 1928 | tf_op jit(solution)/shard_map/ppermute | solution.py:18
  22.1 9.2 %collective-permute-start.5 = (f32[2,16,10,1]{3,2,1,0:T(8,128)S(1)}, f32[2,16,10,1]{3,2,1,0:T(8,128)S(1)}, u32[]{:S(2)}, u32[]{:S(2)}) collective-permute-start(f32[2,16,10,1]{3,2,1,0:T(8,128)S(1)} %get-tuple-element.27), channel_id=1, source_target_pairs={{0,1},{1,2},{2,3},{3,4},{4,5},{5,6},{6,7},{7,8},{8,9},{9,10},{10,1... | collective-permute-start | bytes 3848 | tf_op jit(solution)/shard_map/ppermute | solution.py:17
  26.3 9.2 %collective-permute-start.7 = (f32[2,16,10,1]{3,2,1,0:T(8,128)S(1)}, f32[2,16,10,1]{3,2,1,0:T(8,128)S(1)}, u32[]{:S(2)}, u32[]{:S(2)}) collective-permute-start(f32[2,16,10,1]{3,2,1,0:T(8,128)S(1)} %get-tuple-element.28), channel_id=1, source_target_pairs={{1,0},{2,1},{3,2},{4,3},{5,4},{6,5},{7,6},{8,7},{9,8},{10,9},{11,1... | collective-permute-start | bytes 3848 | tf_op jit(solution)/shard_map/ppermute | solution.py:18
  334.5 4.9 collective-permute-start.8
  337.4 5.1 collective-permute-start.9
  342.7 6.4 collective-permute-start.10
  344.5 8.7 %collective-permute-start.11 = (f32[2,16,10,1]{3,2,1,0:T(8,128)S(1)}, f32[2,16,10,1]{3,2,1,0:T(8,128)S(1)}, u32[]{:S(2)}, u32[]{:S(2)}) collective-permute-start(f32[2,16,10,1]{3,2,1,0:T(8,128)S(1)} %get-tuple-element.26), channel_id=1, source_target_pairs={{1,0},{2,1},{3,2},{4,3},{5,4},{6,5},{7,6},{8,7},{9,8},{10,9},{11,1... | collective-permute-start | bytes 3848 | tf_op jit(solution)/shard_map/ppermute | solution.py:18
  544.1 4.4 collective-permute-start.12
  546.3 5.1 collective-permute-start.13
  551.4 5.2 copy-start.4
  551.5 8.5 %collective-permute-start.14 = (f32[2,16,10,1]{3,2,1,0:T(8,128)S(1)}, f32[2,16,10,1]{3,2,1,0:T(8,128)S(1)}, u32[]{:S(2)}, u32[]{:S(2)}) collective-permute-start(f32[2,16,10,1]{3,2,1,0:T(8,128)S(1)} %get-tuple-element.23), channel_id=1, source_target_pairs={{0,1},{1,2},{2,3},{3,4},{4,5},{5,6},{6,7},{7,8},{8,9},{9,10},{10,1... | collective-permute-start | bytes 3848 | tf_op jit(solution)/shard_map/ppermute | solution.py:17
  555.2 8.9 %collective-permute-start.15 = (f32[2,16,10,1]{3,2,1,0:T(8,128)S(1)}, f32[2,16,10,1]{3,2,1,0:T(8,128)S(1)}, u32[]{:S(2)}, u32[]{:S(2)}) collective-permute-start(f32[2,16,10,1]{3,2,1,0:T(8,128)S(1)} %get-tuple-element.24), channel_id=1, source_target_pairs={{1,0},{2,1},{3,2},{4,3},{5,4},{6,5},{7,6},{8,7},{9,8},{10,9},{11,1... | collective-permute-start | bytes 3848 | tf_op jit(solution)/shard_map/ppermute | solution.py:18
  655.6 23.6 %copy-start = (f32[2,16,8,128]{3,2,1,0:T(8,128)}, f32[2,16,8,128]{3,2,1,0:T(8,128)S(1)}, u32[]{:S(2)}) copy-start(f32[2,16,8,128]{3,2,1,0:T(8,128)S(1)} %multiply_add_fusion) | copy-start | bytes 393220
  655.7 4.4 collective-permute-start.16
  657.6 5.2 collective-permute-start.17
  663.1 11.9 %collective-permute-start.18 = (f32[4,16,10,1]{3,2,1,0:T(8,128)S(1)}, f32[4,16,10,1]{3,2,1,0:T(8,128)S(1)}, u32[]{:S(2)}, u32[]{:S(2)}) collective-permute-start(f32[4,16,10,1]{3,2,1,0:T(8,128)S(1)} %get-tuple-element.19), channel_id=1, source_target_pairs={{0,1},{1,2},{2,3},{3,4},{4,5},{5,6},{6,7},{7,8},{8,9},{9,10},{10,1... | collective-permute-start | bytes 7688 | tf_op jit(solution)/shard_map/ppermute | solution.py:17
  664.6 14.6 %collective-permute-start.19 = (f32[4,16,10,1]{3,2,1,0:T(8,128)S(1)}, f32[4,16,10,1]{3,2,1,0:T(8,128)S(1)}, u32[]{:S(2)}, u32[]{:S(2)}) collective-permute-start(f32[4,16,10,1]{3,2,1,0:T(8,128)S(1)} %get-tuple-element.20), channel_id=1, source_target_pairs={{1,0},{2,1},{3,2},{4,3},{5,4},{6,5},{7,6},{8,7},{9,8},{10,9},{11,1... | collective-permute-start | bytes 7688 | tf_op jit(solution)/shard_map/ppermute | solution.py:18
